TPU v7x, 256 devices: a whole 4x4x8 slice. The times are simulated.
256 devices in a mesh: occ: 64 (over x_hi, y, z), off: 4 (over x_lo, core).
Axes of the slice: x: 4 (x_hi: 2, x_lo: 2; x = x_hi * 2 + x_lo), y: 4, z: 8, core: 2. Of those that a mesh axis runs over, the one named last changes fastest.
Arguments:
- factors: bfloat16 [64, 768, 2048], P('occ'), may hold values from -0.8984375 to 0.8984375
- occ_level: int32 [64], replicated, may hold values from 0 to 255
- vir_level: int32 [768], replicated, may hold values from 0 to 255
- occupied_energy_levels: float32 [256], replicated, may hold values from -2 to -0.5
- vir_table: float32 [256], replicated, may hold values from 0.5 to 4
- virtual_coefficient_matrix: bfloat16 [768, 1024], replicated, may hold values from -0.21875 to 0.21875
Outputs:
- density_ao: float32 [64, 2048, 1024], P(None, ('occ', 'off'))
Inputs may be any that keep to these rules, and one draw needn't show every extreme that they name: `occ_level`: indices into occupied_energy_levels. `vir_level`: indices into vir_table.
All inputs are finite; a program needn't handle non-finite values.
Results may differ from a plain program's by a relative error of at most 0.0032.
Values may be sent and summed in bfloat16 or wider, within the bound.
No kernel may reach another device: no remote copies, remote signals or barrier semaphores. Data moves between devices by JAX's collectives and lax.ppermute only.
A program may use at most 64 MiB of HBM per device.

v0:
```python
import jax
import jax.numpy as jnp
from jax import lax
from jax.sharding import PartitionSpec as P

PAIR_STEPS = 2


def passed_along(value, axis, by):
    length = lax.axis_size(axis)
    return lax.ppermute(value, axis, [(i, (i + by) % length) for i in range(length)])


def lookup(level, table):
    hits = level[:, None] == jnp.arange(table.shape[0], dtype=jnp.int32)[None, :]
    return jnp.sum(jnp.where(hits, table[None, :], jnp.float32(0.0)), axis=1)


def body(
    factors, occ_level, vir_level, occupied_energy_levels, vir_table, virtual_coefficient_matrix
):
    off_count = lax.axis_size("off")
    off_index = lax.axis_index("off")
    occ_count = lax.axis_size("occ")
    occ_index = lax.axis_index("occ")
    vir_energy = lookup(vir_level, vir_table)
    occ_energy = lookup(occ_level, occupied_energy_levels)
    own_energy = lax.dynamic_index_in_dim(occ_energy, occ_index, 0, keepdims=False)
    own = factors[0]
    carried = factors
    moved = factors
    for stride in range(1, off_count):
        moved = passed_along(moved, "occ", 1)
        carried = jnp.where(off_index == stride, moved, carried)
    gamma = jnp.zeros((own.shape[1], own.shape[0]), jnp.float32)
    for step_index in range(PAIR_STEPS):
        offset = off_index + off_count * step_index
        pair_companion = (occ_index - offset) % occ_count
        other_energy = lax.dynamic_index_in_dim(occ_energy, pair_companion, 0, keepdims=False)
        other = carried[0]
        if step_index < PAIR_STEPS - 1:
            carried = passed_along(carried, "occ", off_count)
        integral = lax.dot_general(
            own, other, (((1,), (1,)), ((), ())), preferred_element_type=jnp.float32
        )
        denom = vir_energy[:, None] + vir_energy[None, :] - own_energy - other_energy
        amp = integral / denom
        pair_weight = (2.0 * amp - amp.T).astype(jnp.bfloat16)
        gamma = gamma + lax.dot_general(
            other, pair_weight, (((0,), (1,)), ((), ())), preferred_element_type=jnp.float32
        )
    naux_rows = gamma.shape[0]
    per_device = naux_rows // (occ_count * off_count)
    blocks = gamma.reshape(occ_count, off_count, per_device, gamma.shape[1])
    total = lax.psum(blocks, "off")
    mine = lax.dynamic_slice_in_dim(total, off_index, 1, 1)
    lower_gamma_part = mine.reshape(occ_count, per_device, gamma.shape[1]).astype(jnp.bfloat16)
    finished_flag = jnp.einsum(
        "sbd,dw->sbw",
        lower_gamma_part,
        virtual_coefficient_matrix,
        preferred_element_type=jnp.float32,
    )
    moved_back = lax.all_to_all(finished_flag[None], "occ", split_axis=1, concat_axis=0, tiled=True)
    return moved_back.reshape(moved_back.shape[0], per_device, virtual_coefficient_matrix.shape[1])


def solution(mesh):
    in_specs = (P("occ", None, None), P(), P(), P(), P(), P())
    out_specs = P(None, ("occ", "off"), None)
    return jax.shard_map(body, mesh=mesh, in_specs=in_specs, out_specs=out_specs, check_vma=False)
```

profile of v0, /device:TPU:56, one launch (start us, length us, event | category | flops | bytes accessed | tf_op | source)
XLA Modules:
  0.0 574.3 jit_solution(9931685049981466083)
XLA Ops:
  0.0 0.0 copy-start
  0.0 1.9 collective-permute-start
  1.9 68.1 %collective-permute-done = bf16[1,768,2048]{2,1,0:T(8,128)(2,1)S(1)} collective-permute-done((bf16[1,768,2048]{2,1,0:T(8,128)(2,1)}, bf16[1,768,2048]{2,1,0:T(8,128)(2,1)S(1)}, u32[]{:S(2)}, u32[]{:S(2)}) %collective-permute-start) | collective-permute-done | bytes 3145760 | tf_op jit(solution)/shard_map/ppermute | solution.py:11
  70.1 0.0 copy-start.1
  70.1 1.6 copy-done.1
  71.7 1.9 collective-permute-start.1
  73.6 70.1 %collective-permute-done.1 = bf16[1,768,2048]{2,1,0:T(8,128)(2,1)} collective-permute-done((bf16[1,768,2048]{2,1,0:T(8,128)(2,1)S(1)}, bf16[1,768,2048]{2,1,0:T(8,128)(2,1)}, u32[]{:S(2)}, u32[]{:S(2)}) %collective-permute-start.1) | collective-permute-done | bytes 3145760 | tf_op jit(solution)/shard_map/ppermute | solution.py:11
  143.7 0.0 collective-permute-start.2
  143.7 0.0 copy-start.6
  143.7 0.0 copy-start.7
  143.7 0.0 copy-start.4
  143.7 0.0 copy-start.5
  143.7 70.8 %collective-permute-done.2 = bf16[1,768,2048]{2,1,0:T(8,128)(2,1)} collective-permute-done((bf16[1,768,2048]{2,1,0:T(8,128)(2,1)}, bf16[1,768,2048]{2,1,0:T(8,128)(2,1)}, u32[]{:S(2)}, u32[]{:S(2)}) %collective-permute-start.2) | collective-permute-done | bytes 3145760 | tf_op jit(solution)/shard_map/ppermute | solution.py:11
  214.5 4.1 select_select_fusion
  218.6 2.6 collective-permute-start.3
  221.3 0.0 copy-done.6
  221.3 0.0 copy-done.7
  221.3 0.2 select_reduce_fusion.1
  221.5 0.7 fusion.33
  222.1 0.0 copy-done.4
  222.1 0.0 copy-done.5
  222.1 0.3 select_reduce_fusion
  222.4 6.9 %fusion.5 = f32[768,768]{1,0:T(8,128)} fusion(bf16[1,768,2048]{2,1,0:T(8,128)(2,1)} %param.6, bf16[1,768,2048]{2,1,0:T(8,128)(2,1)} %select_select_fusion), kind=kOutput, calls=%fused_computation.6 | convolution fusion | flops 2415919104 | bytes 8650752 | tf_op jit(solution)/shard_map/dot_general | solution.py:43
  229.3 3.1 copy.14
  232.5 126.0 %collective-permute-done.3 = bf16[1,768,2048]{2,1,0:T(8,128)(2,1)} collective-permute-done((bf16[1,768,2048]{2,1,0:T(8,128)(2,1)}, bf16[1,768,2048]{2,1,0:T(8,128)(2,1)}, u32[]{:S(2)}, u32[]{:S(2)}) %collective-permute-start.3) | collective-permute-done | bytes 3145760 | tf_op jit(solution)/shard_map/ppermute | solution.py:11
  358.4 7.0 %fusion.2 = f32[768,768]{1,0:T(8,128)} fusion(bf16[1,768,2048]{2,1,0:T(8,128)(2,1)} %collective-permute-done.3, bf16[1,768,2048]{2,1,0:T(8,128)(2,1)} %param.6), kind=kOutput, calls=%fused_computation.3 | convolution fusion | flops 2415919104 | bytes 8650752 | tf_op jit(solution)/shard_map/dot_general | solution.py:43
  365.4 3.1 copy.15
  368.5 0.0 copy-start.2
  368.5 0.0 copy-start.3
  368.5 8.3 %fusion = f32[2048,768]{1,0:T(8,128)S(1)} fusion(bf16[1,768,2048]{2,1,0:T(8,128)(2,1)} %collective-permute-done.3, f32[768,768]{0,1:T(8,128)} %copy.15, f32[768,768]{1,0:T(8,128)} %fusion.2, f32[]{:T(128)} %bitcast.7, f32[]{:T(128)} %bitcast.3, f32[768]{0:T(1024)S(1)} %select_reduce_fusion), kind=kOutput, calls=%fused_computation.1 | convolution fusion | flops 2420637696 | bytes 14158856 | tf_op jit(solution)/shard_map/dot_general | solution.py:49
  376.8 0.0 copy-done.2
  376.8 0.0 copy-done.3
  376.8 6.7 %convolution_add_fusion = f32[2048,768]{1,0:T(8,128)S(1)} fusion(f32[2048,768]{1,0:T(8,128)S(1)} %fusion, bf16[1,768,2048]{2,1,0:T(8,128)(2,1)} %select_select_fusion, f32[768,768]{0,1:T(8,128)S(1)} %copy-done.3, f32[768,768]{1,0:T(8,128)S(1)} %copy-done.2, f32[]{:T(128)} %bitcast.4, f32[]{:T(128)} %bitcast.3, f32[768]{0:T(1024)S(1)} %select_reduce_fusion), kind=kOutput, calls=%fused_computation | convolution fusion | flops 2422210560 | bytes 20450312 | tf_op jit(solution)/shard_map/dot_general | solution.py:49
  383.5 3.2 copy.16
  386.7 111.8 %all-reduce.1 = bf16[64,4,8,768]{3,2,0,1:T(8,128)(2,1)} all-reduce(f32[64,4,8,768]{3,2,0,1:T(8,128)} %copy.16), channel_id=1, replica_groups=mesh['occ'=64,'off'=4] {'off'}, use_global_device_ids=true, to_apply=%region_2.3 | all-reduce | flops 1572864 | bytes 9437184 | tf_op jit(solution)/shard_map/psum | solution.py:55
  498.6 0.0 copy-done
  498.6 2.1 convolution_bitcast_fusion
  500.7 72.3 %all_to_all.4 = f32[1,64,8,1024]{3,2,0,1:T(8,128)S(1)} all-to-all(f32[1,64,8,1024]{3,2,0,1:T(8,128)S(1)} %convolution_bitcast_fusion), channel_id=1, replica_groups=mesh['occ'=64,'off'=4] {'occ'}, dimensions={1} | all-to-all | bytes 4194304 | tf_op jit(solution)/shard_map/all_to_all | solution.py:64
  572.9 1.3 copy.21
Async XLA Ops:
  0.0 498.6 %copy-start = (bf16[768,1024]{1,0:T(8,128)(2,1)S(1)}, bf16[768,1024]{1,0:T(8,128)(2,1)}, u32[]{:S(2)}) copy-start(bf16[768,1024]{1,0:T(8,128)(2,1)} %param.11) | copy-start | bytes 4718596
  0.0 70.1 %collective-permute-start = (bf16[1,768,2048]{2,1,0:T(8,128)(2,1)}, bf16[1,768,2048]{2,1,0:T(8,128)(2,1)S(1)}, u32[]{:S(2)}, u32[]{:S(2)}) collective-permute-start(bf16[1,768,2048]{2,1,0:T(8,128)(2,1)} %param.6), channel_id=1, source_target_pairs={{0,4},{4,8},{8,12},{12,16},{16,20},{20,24},{24,28},{28,32},{32,36}... | collective-permute-start | bytes 9437192 | tf_op jit(solution)/shard_map/ppermute | solution.py:11
  70.1 1.6 copy-start.1
  71.7 72.0 %collective-permute-start.1 = (bf16[1,768,2048]{2,1,0:T(8,128)(2,1)S(1)}, bf16[1,768,2048]{2,1,0:T(8,128)(2,1)}, u32[]{:S(2)}, u32[]{:S(2)}) collective-permute-start(bf16[1,768,2048]{2,1,0:T(8,128)(2,1)S(1)} %collective-permute-done), channel_id=1, source_target_pairs={{0,4},{4,8},{8,12},{12,16},{16,20},{20,24},{24,28},{28,32},{32,36}... | collective-permute-start | bytes 9437192 | tf_op jit(solution)/shard_map/ppermute | solution.py:11
  143.7 70.8 %collective-permute-start.2 = (bf16[1,768,2048]{2,1,0:T(8,128)(2,1)}, bf16[1,768,2048]{2,1,0:T(8,128)(2,1)}, u32[]{:S(2)}, u32[]{:S(2)}) collective-permute-start(bf16[1,768,2048]{2,1,0:T(8,128)(2,1)} %collective-permute-done.1), channel_id=1, source_target_pairs={{0,4},{4,8},{8,12},{12,16},{16,20},{20,24},{24,28},{28,32},{32,36}... | collective-permute-start | bytes 9437192 | tf_op jit(solution)/shard_map/ppermute | solution.py:11
  143.7 77.6 %copy-start.6 = (f32[256]{0:T(256)S(1)}, f32[256]{0:T(256)}, u32[]{:S(2)}) copy-start(f32[256]{0:T(256)} %param.9) | copy-start | bytes 3076
  143.7 77.6 %copy-start.7 = (s32[64]{0:T(128)S(1)}, s32[64]{0:T(128)}, u32[]{:S(2)}) copy-start(s32[64]{0:T(128)} %param.7) | copy-start | bytes 772
  143.7 78.4 %copy-start.4 = (s32[768]{0:T(1024)S(1)}, s32[768]{0:T(1024)}, u32[]{:S(2)}) copy-start(s32[768]{0:T(1024)} %param.8) | copy-start | bytes 9220
  143.7 78.4 %copy-start.5 = (f32[256]{0:T(256)S(1)}, f32[256]{0:T(256)}, u32[]{:S(2)}) copy-start(f32[256]{0:T(256)} %param.10) | copy-start | bytes 3076
  218.6 139.8 %collective-permute-start.3 = (bf16[1,768,2048]{2,1,0:T(8,128)(2,1)}, bf16[1,768,2048]{2,1,0:T(8,128)(2,1)}, u32[]{:S(2)}, u32[]{:S(2)}) collective-permute-start(bf16[1,768,2048]{2,1,0:T(8,128)(2,1)} %select_select_fusion), channel_id=1, source_target_pairs={{0,16},{4,20},{8,24},{12,28},{16,32},{20,36},{24,40},{28,44},{32,4... | collective-permute-start | bytes 9437192 | tf_op jit(solution)/shard_map/ppermute | solution.py:11
  368.5 8.3 %copy-start.2 = (f32[768,768]{1,0:T(8,128)S(1)}, f32[768,768]{1,0:T(8,128)}, u32[]{:S(2)}) copy-start(f32[768,768]{1,0:T(8,128)} %fusion.5) | copy-start | bytes 7077892
  368.5 8.3 %copy-start.3 = (f32[768,768]{0,1:T(8,128)S(1)}, f32[768,768]{0,1:T(8,128)}, u32[]{:S(2)}) copy-start(f32[768,768]{0,1:T(8,128)} %copy.14) | copy-start | bytes 7077892
where the time goes:
time: 575 us; the launch traced here: 574 us
  waiting for transfers between devices  335 us (58%)
  blocking collectives  184 us (32%)
  matrix products  31 us (5%)
  local copies, waits for them, and re-layouts  13.1 us (2%)
  starting transfers between devices  6.48 us (1%)
    ppermute x4, waiting for transfers between devices, passed_along(): lax.ppermute(value, axis, [(i, (i + by) % length) for i in range(length)])  335 us
    psum x1, blocking collectives, body(): total = lax.psum(blocks, 'off')  112 us
    all_to_all x1, blocking collectives, body(): lax.all_to_all(finished_flag[None], 'occ', split_axis=1, concat_axis=0, t...  72.3 us
    dot_general x2, matrix products, body(): lax.dot_general(other, pair_weight, (((0,), (1,)), ((), ())), preferred_e...  15 us
    dot_general x2, matrix products, body(): lax.dot_general(own, other, (((1,), (1,)), ((), ())), preferred_element_t...  13.9 us
  transfers between devices with their start and end apart: 4, of which 4 were waited for; matrix products, arithmetic and copies ran while one was open for 2% of the time, Pallas kernels for 0%

commit v1 on v0

--- a/solution.py
+++ b/solution.py
@@ -52,7 +52,7 @@
     naux_rows = gamma.shape[0]
     per_device = naux_rows // (occ_count * off_count)
     blocks = gamma.reshape(occ_count, off_count, per_device, gamma.shape[1])
-    total = lax.psum(blocks, "off")
+    total = jnp.sum(lax.all_gather(blocks, "off"), axis=0)
     mine = lax.dynamic_slice_in_dim(total, off_index, 1, 1)
     lower_gamma_part = mine.reshape(occ_count, per_device, gamma.shape[1]).astype(jnp.bfloat16)
     finished_flag = jnp.einsum(

time: 575 us -> 715 us (1.24)
  waiting for transfers between devices: 335 us -> 567 us
  blocking collectives: 184 us -> 66.4 us
  between operations: 0.08 us -> 13.5 us
  other arithmetic: 4.54 us -> 16.9 us
    all_gather x0 -> x1, waiting for transfers between devices: none -> 232 us  [body(): total = jnp.sum(lax.all_gather(blocks, 'off'), axis=0)]
    psum x1 -> x0, blocking collectives: 112 us -> none  [body(): total = lax.psum(blocks, 'off')]
    reduce_sum x0 -> x1, other arithmetic: none -> 12.4 us  [body(): total = jnp.sum(lax.all_gather(blocks, 'off'), axis=0)]
  transfers between devices with their start and end apart: 4 -> 5, of which waited for: 4 -> 5; matrix products, arithmetic and copies ran while one was open for 2% -> 2% of each run, Pallas kernels for 0% -> 0%
where the time goes in v1:
time: 715 us; the launch traced here: 714 us
  waiting for transfers between devices  567 us (79%)
  blocking collectives  66.4 us (9%)
  matrix products  33.9 us (5%)
  other arithmetic  16.9 us (2%)
  between operations  13.5 us (2%)
  local copies, waits for them, and re-layouts  9.8 us (1%)
    ppermute x4, waiting for transfers between devices, passed_along(): lax.ppermute(value, axis, [(i, (i + by) % length) for i in range(length)])  335 us
    all_gather x1, waiting for transfers between devices, body(): total = jnp.sum(lax.all_gather(blocks, 'off'), axis=0)  232 us
    all_to_all x1, blocking collectives, body(): lax.all_to_all(finished_flag[None], 'occ', split_axis=1, concat_axis=0, t...  66.4 us
    dot_general x2, matrix products, body(): lax.dot_general(other, pair_weight, (((0,), (1,)), ((), ())), preferred_e...  17.8 us
  transfers between devices with their start and end apart: 5, of which 5 were waited for; matrix products, arithmetic and copies ran while one was open for 2% of the time, Pallas kernels for 0%

profile of v1, /device:TPU:56, one launch (start us, length us, event | category | flops | bytes accessed | tf_op | source)
XLA Modules:
  0.0 713.6 jit_solution(6589051798578993189)
XLA Ops:
  6.5 0.0 copy-start
  6.5 0.0 all-gather.2.cloned.1.call-start
  6.5 1.9 collective-permute-start
  8.5 68.1 %collective-permute-done = bf16[1,768,2048]{2,1,0:T(8,128)(2,1)S(1)} collective-permute-done((bf16[1,768,2048]{2,1,0:T(8,128)(2,1)}, bf16[1,768,2048]{2,1,0:T(8,128)(2,1)S(1)}, u32[]{:S(2)}, u32[]{:S(2)}) %collective-permute-start) | collective-permute-done | bytes 3145760 | tf_op jit(solution)/shard_map/ppermute | solution.py:11
  76.6 0.0 copy-start.1
  76.6 1.6 copy-done.1
  78.2 1.9 collective-permute-start.1
  80.2 70.1 %collective-permute-done.1 = bf16[1,768,2048]{2,1,0:T(8,128)(2,1)} collective-permute-done((bf16[1,768,2048]{2,1,0:T(8,128)(2,1)S(1)}, bf16[1,768,2048]{2,1,0:T(8,128)(2,1)}, u32[]{:S(2)}, u32[]{:S(2)}) %collective-permute-start.1) | collective-permute-done | bytes 3145760 | tf_op jit(solution)/shard_map/ppermute | solution.py:11
  150.3 0.0 collective-permute-start.2
  150.3 0.0 copy-start.6
  150.3 0.0 copy-start.7
  150.3 0.0 copy-start.4
  150.3 0.0 copy-start.5
  150.3 70.8 %collective-permute-done.2 = bf16[1,768,2048]{2,1,0:T(8,128)(2,1)} collective-permute-done((bf16[1,768,2048]{2,1,0:T(8,128)(2,1)}, bf16[1,768,2048]{2,1,0:T(8,128)(2,1)}, u32[]{:S(2)}, u32[]{:S(2)}) %collective-permute-start.2) | collective-permute-done | bytes 3145760 | tf_op jit(solution)/shard_map/ppermute | solution.py:11
  221.1 4.1 select_select_fusion
  225.2 2.6 collective-permute-start.3
  227.8 0.0 copy-done.6
  227.8 0.0 copy-done.7
  227.8 0.2 select_reduce_fusion.1
  228.0 0.6 fusion.33
  228.6 0.0 copy-done.4
  228.6 0.0 copy-done.5
  228.6 0.3 select_reduce_fusion
  228.9 6.9 fusion.5
  235.9 3.1 copy.13
  239.0 126.0 %collective-permute-done.3 = bf16[1,768,2048]{2,1,0:T(8,128)(2,1)} collective-permute-done((bf16[1,768,2048]{2,1,0:T(8,128)(2,1)}, bf16[1,768,2048]{2,1,0:T(8,128)(2,1)}, u32[]{:S(2)}, u32[]{:S(2)}) %collective-permute-start.3) | collective-permute-done | bytes 3145760 | tf_op jit(solution)/shard_map/ppermute | solution.py:11
  365.0 7.0 fusion.2
  372.0 3.1 copy.14
  375.1 0.0 copy-start.2
  375.1 0.0 copy-start.3
  375.1 8.3 %fusion = f32[2048,768]{1,0:T(8,128)S(1)} fusion(bf16[1,768,2048]{2,1,0:T(8,128)(2,1)} %collective-permute-done.3, f32[768,768]{0,1:T(8,128)} %copy.14, f32[768,768]{1,0:T(8,128)} %fusion.2, f32[]{:T(128)} %bitcast.7, f32[]{:T(128)} %bitcast.3, f32[768]{0:T(1024)S(1)} %select_reduce_fusion), kind=kOutput, calls=%fused_computation.1 | convolution fusion | flops 2420637696 | bytes 14158856 | tf_op jit(solution)/shard_map/dot_general | solution.py:49
  383.4 0.0 copy-done.2
  383.4 0.0 copy-done.3
  383.4 9.5 %convolution_add_fusion = f32[2048,768]{1,0:T(8,128)} fusion(f32[2048,768]{1,0:T(8,128)S(1)} %fusion, bf16[1,768,2048]{2,1,0:T(8,128)(2,1)} %select_select_fusion, f32[768,768]{0,1:T(8,128)S(1)} %copy-done.3, f32[768,768]{1,0:T(8,128)S(1)} %copy-done.2, f32[]{:T(128)} %bitcast.4, f32[]{:T(128)} %bitcast.3, f32[768]{0:T(1024)S(1)} %select_reduce_fusion), kind=kOutput, calls=%fused_computation | convolution fusion | flops 2422210560 | bytes 20450312 | tf_op jit(solution)/shard_map/dot_general | solution.py:49
  392.9 0.0 all-gather.2.cloned.1.call-update
  392.9 231.6 %all-gather.2.cloned.1.call-done = f32[4,64,4,8,768]{4,3,2,1,0:T(8,128)} async-done(((f32[1,64,4,8,768]{4,3,2,1,0:T(8,128)}), f32[4,64,4,8,768]{4,3,2,1,0:T(8,128)}) %all-gather.2.cloned.1.call-update) | async-done | bytes 25165840 | tf_op jit(solution)/shard_map/all_gather | solution.py:55
  624.5 12.4 %reduce_sum.29 = bf16[64,4,8,768]{3,2,1,0:T(8,128)(2,1)} reduce(f32[4,64,4,8,768]{4,3,2,1,0:T(8,128)} %all-gather.2.cloned.1.call-done, f32[]{:T(128)} %constant.39.clone.1), dimensions={0}, to_apply=%region_2.3 | reduce | flops 4718592 | bytes 28311556 | tf_op jit(solution)/shard_map/reduce_sum | solution.py:55
  636.9 0.0 copy-done
  636.9 2.1 convolution_bitcast_fusion
  639.0 66.4 %all_to_all.4 = f32[1,64,8,1024]{3,2,0,1:T(8,128)S(1)} all-to-all(f32[1,64,8,1024]{3,2,0,1:T(8,128)S(1)} %convolution_bitcast_fusion), channel_id=1, replica_groups=mesh['occ'=64,'off'=4] {'occ'}, dimensions={1} | all-to-all | bytes 4194304 | tf_op jit(solution)/shard_map/all_to_all | solution.py:64
  705.4 1.3 copy.19
Async XLA Ops:
  6.5 630.4 %copy-start = (bf16[768,1024]{1,0:T(8,128)(2,1)S(1)}, bf16[768,1024]{1,0:T(8,128)(2,1)}, u32[]{:S(2)}) copy-start(bf16[768,1024]{1,0:T(8,128)(2,1)} %param.11) | copy-start | bytes 4718596
  6.5 618.0 %all-gather.2.cloned.1.call-start = ((), (), s32[]{:S(2)}) async-start(), calls=%async_computation.1 | async-start | bytes 31457280 | tf_op jit(solution)/shard_map/all_gather | solution.py:55
  6.5 70.1 %collective-permute-start = (bf16[1,768,2048]{2,1,0:T(8,128)(2,1)}, bf16[1,768,2048]{2,1,0:T(8,128)(2,1)S(1)}, u32[]{:S(2)}, u32[]{:S(2)}) collective-permute-start(bf16[1,768,2048]{2,1,0:T(8,128)(2,1)} %param.6), channel_id=1, source_target_pairs={{0,4},{4,8},{8,12},{12,16},{16,20},{20,24},{24,28},{28,32},{32,36}... | collective-permute-start | bytes 9437192 | tf_op jit(solution)/shard_map/ppermute | solution.py:11
  76.6 1.7 copy-start.1
  78.2 72.0 %collective-permute-start.1 = (bf16[1,768,2048]{2,1,0:T(8,128)(2,1)S(1)}, bf16[1,768,2048]{2,1,0:T(8,128)(2,1)}, u32[]{:S(2)}, u32[]{:S(2)}) collective-permute-start(bf16[1,768,2048]{2,1,0:T(8,128)(2,1)S(1)} %collective-permute-done), channel_id=1, source_target_pairs={{0,4},{4,8},{8,12},{12,16},{16,20},{20,24},{24,28},{28,32},{32,36}... | collective-permute-start | bytes 9437192 | tf_op jit(solution)/shard_map/ppermute | solution.py:11
  150.3 70.8 %collective-permute-start.2 = (bf16[1,768,2048]{2,1,0:T(8,128)(2,1)}, bf16[1,768,2048]{2,1,0:T(8,128)(2,1)}, u32[]{:S(2)}, u32[]{:S(2)}) collective-permute-start(bf16[1,768,2048]{2,1,0:T(8,128)(2,1)} %collective-permute-done.1), channel_id=1, source_target_pairs={{0,4},{4,8},{8,12},{12,16},{16,20},{20,24},{24,28},{28,32},{32,36}... | collective-permute-start | bytes 9437192 | tf_op jit(solution)/shard_map/ppermute | solution.py:11
  150.3 77.6 %copy-start.6 = (f32[256]{0:T(256)S(1)}, f32[256]{0:T(256)}, u32[]{:S(2)}) copy-start(f32[256]{0:T(256)} %param.9) | copy-start | bytes 3076
  150.3 77.6 %copy-start.7 = (s32[64]{0:T(128)S(1)}, s32[64]{0:T(128)}, u32[]{:S(2)}) copy-start(s32[64]{0:T(128)} %param.7) | copy-start | bytes 772
  150.3 78.4 %copy-start.4 = (s32[768]{0:T(1024)S(1)}, s32[768]{0:T(1024)}, u32[]{:S(2)}) copy-start(s32[768]{0:T(1024)} %param.8) | copy-start | bytes 9220
  150.3 78.4 %copy-start.5 = (f32[256]{0:T(256)S(1)}, f32[256]{0:T(256)}, u32[]{:S(2)}) copy-start(f32[256]{0:T(256)} %param.10) | copy-start | bytes 3076
  225.2 139.8 %collective-permute-start.3 = (bf16[1,768,2048]{2,1,0:T(8,128)(2,1)}, bf16[1,768,2048]{2,1,0:T(8,128)(2,1)}, u32[]{:S(2)}, u32[]{:S(2)}) collective-permute-start(bf16[1,768,2048]{2,1,0:T(8,128)(2,1)} %select_select_fusion), channel_id=1, source_target_pairs={{0,16},{4,20},{8,24},{12,28},{16,32},{20,36},{24,40},{28,44},{32,4... | collective-permute-start | bytes 9437192 | tf_op jit(solution)/shard_map/ppermute | solution.py:11
  375.1 8.3 %copy-start.2 = (f32[768,768]{1,0:T(8,128)S(1)}, f32[768,768]{1,0:T(8,128)}, u32[]{:S(2)}) copy-start(f32[768,768]{1,0:T(8,128)} %fusion.5) | copy-start | bytes 7077892
  375.1 8.3 %copy-start.3 = (f32[768,768]{0,1:T(8,128)S(1)}, f32[768,768]{0,1:T(8,128)}, u32[]{:S(2)}) copy-start(f32[768,768]{0,1:T(8,128)} %copy.13) | copy-start | bytes 7077892
Sparse Core Ops, SparseCore 0:
  393.1 231.4 all-gather.1
